TPU v7x, 32 devices: a whole 2x2x4 slice. The times are simulated.
32 devices in a mesh: row: 8 (over z, y), col: 4 (over x, core).
Axes of the slice: x: 2, y: 2, z: 4, core: 2. Of those that a mesh axis runs over, the one named last changes fastest.
Arguments:
- three_index: bfloat16 [8, 4, 8, 2, 128, 128], P('row', 'col'), may hold values from -6 to 6
- slot_pair: int32 [8, 4, 8], P('row', 'col'), may hold values from -1 to 31, as said below
- coeff: bfloat16 [4096, 256], P(('col', 'row')), may hold values from -0.125 to 0.125
- occ_mask: int32 [32, 2], P('col'), may hold values 0 or 1
Outputs:
- exchange_block: bfloat16 [4096, 4096], P('row', 'col')
Inputs may be any that keep to these rules, and one draw needn't show every extreme that they name: `slot_pair`: on each device (first two dimensions) the 8 slots name distinct local pair blocks mb * 8 + nb, the live ones first and -1 after them; in every draw some device fills all 8 slots.
All inputs are finite; a program needn't handle non-finite values. No bound on the sum of `occ_mask` on one device may be relied on, other than what follows from the above.
Results may differ from a plain program's by a relative error of at most 0.0057.
Values may be sent and summed in bfloat16 or wider, within the bound.
No kernel may reach another device: no remote copies, remote signals or barrier semaphores. Data moves between devices by JAX's collectives and lax.ppermute only.
A program may use at most 64 MiB of HBM per device.

v0:
```python
import jax
import jax.numpy as jnp
from jax import lax
from jax.sharding import PartitionSpec as P

MB_DEV = 4


def spread(value, axis, root):
    mine = lax.axis_index(axis) == root
    return lax.psum(jnp.where(mine, value, jnp.zeros_like(value)), axis)


def body(three_index, slot_pair, coeff, occ_mask):
    block_size = three_index.shape[4]
    aux_count = three_index.shape[3]
    occ_count = coeff.shape[1]
    gathered = lax.all_gather(coeff, "row", axis=0, tiled=True)
    nu_blocks = gathered.shape[0] // block_size
    occ_blocks = occ_count // block_size
    keep = occ_mask.astype(jnp.bfloat16)[:, None, :, None]
    masked = (gathered.reshape(nu_blocks, block_size, occ_blocks, block_size) * keep).reshape(
        gathered.shape[0], occ_count
    )
    blocks = three_index[0, 0]
    slots = slot_pair[0, 0]
    mu_rows_count = MB_DEV * block_size
    live_count = jnp.sum((slots >= 0).astype(jnp.int32))

    def add_slot(slot_index, partial_value):
        pair = slots[slot_index]
        mu_start = pair // nu_blocks * block_size
        nu_start = pair % nu_blocks * block_size
        rows = lax.dynamic_slice_in_dim(masked, nu_start, block_size, 0)
        term = jnp.einsum(
            "pab,bi->api", blocks[slot_index], rows, preferred_element_type=jnp.float32
        )
        current = lax.dynamic_slice_in_dim(partial_value, mu_start, block_size, 0)
        return lax.dynamic_update_slice_in_dim(partial_value, current + term, mu_start, 0)

    partial_value = jnp.zeros((mu_rows_count, aux_count, occ_count), jnp.float32)
    partial_value = lax.fori_loop(0, live_count, add_slot, partial_value)
    ratio = lax.axis_size("row") // lax.axis_size("col")
    col_place = lax.axis_index("col")
    mu_half = lax.psum(partial_value, "col").astype(jnp.bfloat16)
    pieces = []
    for mirror in range(ratio):
        pieces.append(spread(mu_half, "row", ratio * col_place + mirror))
    nu_half = jnp.concatenate(pieces, 0)
    left = mu_half.reshape(mu_rows_count, aux_count * occ_count)
    right = nu_half.reshape(nu_half.shape[0], aux_count * occ_count)
    product = lax.dot_general(
        left, right, (((1,), (1,)), ((), ())), preferred_element_type=jnp.float32
    )
    return (product / jnp.sqrt(jnp.float32(aux_count * occ_count))).astype(jnp.bfloat16)


def solution(mesh):
    return jax.shard_map(
        body,
        mesh=mesh,
        in_specs=(
            P("row", "col", None, None, None, None),
            P("row", "col", None),
            P(("col", "row"), None),
            P("col", None),
        ),
        out_specs=P("row", "col"),
        check_vma=False,
    )
```

profile of v0, /device:TPU:0, one launch (start us, length us, event | category | flops | bytes accessed | tf_op | source)
XLA Modules:
  0.0 192.0 jit_solution(16867687880733982412)
XLA Ops:
  6.5 1.4 fusion.10
  7.9 0.7 convert_element_type.13
  8.6 0.9 copy.5
  9.5 29.6 %all_gather.3 = bf16[1024,256]{0,1:T(8,128)(2,1)S(1)} all-gather(bf16[128,256]{0,1:T(8,128)(2,1)S(1)} %copy.5), channel_id=1, replica_groups=mesh['row'=8,'col'=4] {'row'}, dimensions={0}, use_global_device_ids=true | all-gather | bytes 589824 | tf_op jit(solution)/shard_map/all_gather | solution.py:18
  39.1 0.1 mul.27
  39.2 0.1 bitcast_multiply_fusion.1
  39.4 0.5 copy-done
  39.9 15.5 %while.12 = (s32[]{:T(128)}, f32[512,2,256]{2,0,1:T(8,128)S(1)}, s32[]{:T(128)}, s32[8]{0:T(128)S(1)}, bf16[1024,256]{0,1:T(8,128)(2,1)S(1)}, /*index=5*/bf16[8,...) while((s32[]{:T(128)}, f32[512,2,256]{2,0,1:T(8,128)S(1)}, ...), condition=%wide.region_2.3_spmd, body=%wide.region_1.2_spmd.sunk | while | flops 16842784 | bytes 2753002 | solution.py:42
  40.6 0.6 dynamic_slice.40
  43.5 0.1 copy.14
  43.6 1.0 fusion.19
  44.6 0.1 copy.15
  45.5 0.6 dynamic_slice.40
  48.4 0.1 copy.14
  48.5 1.0 fusion.19
  49.6 0.1 copy.15
  50.5 0.6 dynamic_slice.40
  53.3 0.1 copy.14
  53.5 1.0 fusion.19
  54.5 0.1 copy.15
  55.4 50.0 %all-reduce.5 = bf16[512,2,256]{2,0,1:T(8,128)(2,1)S(1)} all-reduce(f32[512,2,256]{2,0,1:T(8,128)S(1)} %get-tuple-element.88), channel_id=1, replica_groups=mesh['row'=8,'col'=4] {'col'}, use_global_device_ids=true, to_apply=%region_3.4 | all-reduce | flops 262144 | bytes 1572864 | tf_op jit(solution)/shard_map/psum | solution.py:45
  105.4 1.1 broadcast_select_fusion.1
  106.5 75.7 %all-reduce.4.cloned.1.call-done = (bf16[512,2,256]{2,0,1:T(8,128)(2,1)}, bf16[512,2,256]{2,0,1:T(8,128)(2,1)}) async-done(((bf16[512,2,256]{2,0,1:T(8,128)(2,1)}, bf16[512,2,256]{2,0,1:T(8,128)(2,1)}), (bf16[512,2,256]{2,0,1:T(8,128)(2,1)}, bf16[512,2,256]{2,0,1:T(8,128)(2,1)})) %all-reduce.4.cloned.1.call-update) | async-done | bytes 1048592 | tf_op jit(solution)/shard_map/psum | solution.py:11
  182.3 2.9 %fusion.6 = bf16[512,1024]{1,0:T(8,128)(2,1)} fusion(bf16[512,2,256]{2,0,1:T(8,128)(2,1)} %get-tuple-element.101, bf16[512,2,256]{2,0,1:T(8,128)(2,1)} %get-tuple-element.102, bf16[512,2,256]{2,0,1:T(8,128)(2,1)S(1)} %all-reduce.5), kind=kOutput, calls=%fused_computation.10 | convolution fusion | flops 540016640 | bytes 2621440 | tf_op jit(solution)/shard_map/dot_general | solution.py:52
  (10 shorter events, 0.2 us)
Async XLA Ops:
  6.5 175.7 %all-reduce.4.cloned.1.call-start = ((), (), s32[]{:S(2)}) async-start(), calls=%async_computation | async-start | bytes 2097152 | tf_op jit(solution)/shard_map/psum | solution.py:11
  39.2 0.7 copy-start
Sparse Core Ops, SparseCore 0:
  106.6 75.5 all-reduce.3
where the time goes:
time: 193 us; the launch traced here: 192 us
  blocking collectives  79.6 us (41%)
  waiting for transfers between devices  75.8 us (39%)
  between operations  13.4 us (7%)
  loops' own time  9.75 us (5%)
  matrix products  6.01 us (3%)
  local copies, waits for them, and re-layouts  4.25 us (2%)
  other arithmetic  3.19 us (2%)
    psum x1, waiting for transfers between devices, spread(): return lax.psum(jnp.where(mine, value, jnp.zeros_like(value)), axis)  75.7 us
    psum x1, blocking collectives, body(): mu_half = lax.psum(partial_value, 'col').astype(jnp.bfloat16)  50 us
    all_gather x1, blocking collectives, body(): gathered = lax.all_gather(coeff, 'row', axis=0, tiled=True)  29.6 us
    another operation x1, loops' own time, body(): partial_value = lax.fori_loop(0, live_count, add_slot, partial_value)  9.75 us
  transfers between devices with their start and end apart: 1, of which 1 were waited for; matrix products, arithmetic and copies ran while one was open for 0% of the time, Pallas kernels for 0%

commit v1 on v0

--- a/solution.py
+++ b/solution.py
@@ -15,7 +15,14 @@
     block_size = three_index.shape[4]
     aux_count = three_index.shape[3]
     occ_count = coeff.shape[1]
-    gathered = lax.all_gather(coeff, "row", axis=0, tiled=True)
+    size = lax.axis_size("row")
+    route = [(i, (i + 1) % size) for i in range(size)]
+    parts = [coeff]
+    for hop in range(1, size):
+        parts = [lax.ppermute(parts[0], "row", route), *parts]
+    whole = jnp.concatenate(parts, axis=0)
+    shift = (lax.axis_index("row") + 1) * parts[-1].shape[0]
+    gathered = jnp.roll(whole, shift, axis=0)
     nu_blocks = gathered.shape[0] // block_size
     occ_blocks = occ_count // block_size
     keep = occ_mask.astype(jnp.bfloat16)[:, None, :, None]

time: 193 us -> 212 us (1.098)
  waiting for transfers between devices: 75.8 us -> 121 us
  blocking collectives: 79.6 us -> 50.4 us
  starting transfers between devices: 0.01 us -> 3.07 us
    ppermute x0 -> x7, waiting for transfers between devices: none -> 45.3 us  [body(): parts = [lax.ppermute(parts[0], 'row', route), *parts]]
    all_gather x1 -> x0, blocking collectives: 29.6 us -> none  [body(): gathered = lax.all_gather(coeff, 'row', axis=0, tiled=True)]
    ppermute x0 -> x7, starting transfers between devices: none -> 3.06 us  [body(): parts = [lax.ppermute(parts[0], 'row', route), *parts]]
  transfers between devices with their start and end apart: 1 -> 8, of which waited for: 1 -> 8; matrix products, arithmetic and copies ran while one was open for 0% -> 1% of each run, Pallas kernels for 0% -> 0%
where the time goes in v1:
time: 212 us
  waiting for transfers between devices  121 us (57%)
  blocking collectives  50.4 us (24%)
  between operations  13.5 us (6%)
  loops' own time  9.77 us (5%)
  matrix products  6.01 us (3%)
  local copies, waits for them, and re-layouts  4.42 us (2%)
  other arithmetic  3.31 us (2%)
  starting transfers between devices  3.07 us (1%)
    psum x1, waiting for transfers between devices, spread(): return lax.psum(jnp.where(mine, value, jnp.zeros_like(value)), axis)  75.6 us
    psum x1, blocking collectives, body(): mu_half = lax.psum(partial_value, 'col').astype(jnp.bfloat16)  50.4 us
    ppermute x7, waiting for transfers between devices, body(): parts = [lax.ppermute(parts[0], 'row', route), *parts]  45.3 us
    another operation x1, loops' own time, body(): partial_value = lax.fori_loop(0, live_count, add_slot, partial_value)  9.77 us
  transfers between devices with their start and end apart: 8, of which 8 were waited for; matrix products, arithmetic and copies ran while one was open for 1% of the time, Pallas kernels for 0%

profile of v1, /device:TPU:0, one launch (start us, length us, event | category | flops | bytes accessed | tf_op | source)
XLA Modules:
  0.0 211.5 jit_solution(941608245201623549)
XLA Ops:
  6.5 0.9 copy.5
  7.5 3.0 %collective-permute-start = (bf16[128,256]{0,1:T(8,128)(2,1)S(1)}, bf16[128,256]{0,1:T(8,128)(2,1)S(1)}, u32[]{:S(2)}, u32[]{:S(2)}) collective-permute-start(bf16[128,256]{0,1:T(8,128)(2,1)S(1)} %copy.5), channel_id=1, source_target_pairs={{0,4},{4,8},{8,12},{12,16},{16,20},{20,24},{24,28},{28,0},{1,5},{5... | collective-permute-start | bytes 196616 | tf_op jit(solution)/shard_map/ppermute | solution.py:22
  10.5 5.3 %collective-permute-done = bf16[128,256]{0,1:T(8,128)(2,1)S(1)} collective-permute-done((bf16[128,256]{0,1:T(8,128)(2,1)S(1)}, bf16[128,256]{0,1:T(8,128)(2,1)S(1)}, u32[]{:S(2)}, u32[]{:S(2)}) %collective-permute-start) | collective-permute-done | bytes 65568 | tf_op jit(solution)/shard_map/ppermute | solution.py:22
  15.8 7.0 %collective-permute-done.1 = bf16[128,256]{0,1:T(8,128)(2,1)S(1)} collective-permute-done((bf16[128,256]{0,1:T(8,128)(2,1)S(1)}, bf16[128,256]{0,1:T(8,128)(2,1)S(1)}, u32[]{:S(2)}, u32[]{:S(2)}) %collective-permute-start.1) | collective-permute-done | bytes 65568 | tf_op jit(solution)/shard_map/ppermute | solution.py:22
  22.8 7.0 %collective-permute-done.2 = bf16[128,256]{0,1:T(8,128)(2,1)S(1)} collective-permute-done((bf16[128,256]{0,1:T(8,128)(2,1)S(1)}, bf16[128,256]{0,1:T(8,128)(2,1)S(1)}, u32[]{:S(2)}, u32[]{:S(2)}) %collective-permute-start.2) | collective-permute-done | bytes 65568 | tf_op jit(solution)/shard_map/ppermute | solution.py:22
  29.8 7.0 %collective-permute-done.3 = bf16[128,256]{0,1:T(8,128)(2,1)S(1)} collective-permute-done((bf16[128,256]{0,1:T(8,128)(2,1)S(1)}, bf16[128,256]{0,1:T(8,128)(2,1)S(1)}, u32[]{:S(2)}, u32[]{:S(2)}) %collective-permute-start.3) | collective-permute-done | bytes 65568 | tf_op jit(solution)/shard_map/ppermute | solution.py:22
  36.7 7.3 %collective-permute-done.4 = bf16[128,256]{0,1:T(8,128)(2,1)S(1)} collective-permute-done((bf16[128,256]{0,1:T(8,128)(2,1)S(1)}, bf16[128,256]{0,1:T(8,128)(2,1)S(1)}, u32[]{:S(2)}, u32[]{:S(2)}) %collective-permute-start.4) | collective-permute-done | bytes 65568 | tf_op jit(solution)/shard_map/ppermute | solution.py:22
  44.0 0.7 convert_element_type.13
  44.7 6.3 %collective-permute-done.5 = bf16[128,256]{0,1:T(8,128)(2,1)S(1)} collective-permute-done((bf16[128,256]{0,1:T(8,128)(2,1)S(1)}, bf16[128,256]{0,1:T(8,128)(2,1)S(1)}, u32[]{:S(2)}, u32[]{:S(2)}) %collective-permute-start.5) | collective-permute-done | bytes 65568 | tf_op jit(solution)/shard_map/ppermute | solution.py:22
  51.0 1.4 fusion.10
  52.4 5.6 %collective-permute-done.6 = bf16[128,256]{0,1:T(8,128)(2,1)S(1)} collective-permute-done((bf16[128,256]{0,1:T(8,128)(2,1)S(1)}, bf16[128,256]{0,1:T(8,128)(2,1)S(1)}, u32[]{:S(2)}, u32[]{:S(2)}) %collective-permute-start.6) | collective-permute-done | bytes 65568 | tf_op jit(solution)/shard_map/ppermute | solution.py:22
  58.5 0.2 bitcast_multiply_fusion.1
  58.8 0.4 copy-done
  59.1 15.5 %while.12 = (s32[]{:T(128)}, f32[512,2,256]{2,0,1:T(8,128)S(1)}, s32[]{:T(128)}, s32[8]{0:T(128)S(1)}, bf16[1024,256]{0,1:T(8,128)(2,1)S(1)}, /*index=5*/bf16[8,...) while((s32[]{:T(128)}, f32[512,2,256]{2,0,1:T(8,128)S(1)}, ...), condition=%wide.region_2.3_spmd, body=%wide.region_1.2_spmd.sunk | while | flops 16842784 | bytes 2752994 | solution.py:49
  59.8 0.6 dynamic_slice.46
  62.8 1.0 fusion.19
  64.8 0.6 dynamic_slice.46
  67.8 1.0 fusion.19
  69.7 0.6 dynamic_slice.46
  72.7 1.0 fusion.19
  74.6 50.4 %all-reduce.5 = bf16[512,2,256]{2,0,1:T(8,128)(2,1)S(1)} all-reduce(f32[512,2,256]{2,0,1:T(8,128)S(1)} %get-tuple-element.88), channel_id=1, replica_groups=mesh['row'=8,'col'=4] {'col'}, use_global_device_ids=true, to_apply=%region_3.4 | all-reduce | flops 262144 | bytes 1572864 | tf_op jit(solution)/shard_map/psum | solution.py:52
  125.0 1.1 broadcast_select_fusion.1
  126.1 75.6 %all-reduce.4.cloned.1.call-done = (bf16[512,2,256]{2,0,1:T(8,128)(2,1)}, bf16[512,2,256]{2,0,1:T(8,128)(2,1)}) async-done(((bf16[512,2,256]{2,0,1:T(8,128)(2,1)}, bf16[512,2,256]{2,0,1:T(8,128)(2,1)}), (bf16[512,2,256]{2,0,1:T(8,128)(2,1)}, bf16[512,2,256]{2,0,1:T(8,128)(2,1)})) %all-reduce.4.cloned.1.call-update) | async-done | bytes 1048592 | tf_op jit(solution)/shard_map/psum | solution.py:11
  201.8 2.9 %fusion.6 = bf16[512,1024]{1,0:T(8,128)(2,1)} fusion(bf16[512,2,256]{2,0,1:T(8,128)(2,1)} %get-tuple-element.101, bf16[512,2,256]{2,0,1:T(8,128)(2,1)} %get-tuple-element.102, bf16[512,2,256]{2,0,1:T(8,128)(2,1)S(1)} %all-reduce.5), kind=kOutput, calls=%fused_computation.10 | convolution fusion | flops 540016640 | bytes 2621440 | tf_op jit(solution)/shard_map/dot_general | solution.py:59
  (39 shorter events, 1.4 us)
Async XLA Ops:
  6.5 195.2 %all-reduce.4.cloned.1.call-start = ((), (), s32[]{:S(2)}) async-start(), calls=%async_computation | async-start | bytes 2097152 | tf_op jit(solution)/shard_map/psum | solution.py:11
  7.5 8.3 %collective-permute-start = (bf16[128,256]{0,1:T(8,128)(2,1)S(1)}, bf16[128,256]{0,1:T(8,128)(2,1)S(1)}, u32[]{:S(2)}, u32[]{:S(2)}) collective-permute-start(bf16[128,256]{0,1:T(8,128)(2,1)S(1)} %copy.5), channel_id=1, source_target_pairs={{0,4},{4,8},{8,12},{12,16},{16,20},{20,24},{24,28},{28,0},{1,5},{5... | collective-permute-start | bytes 196616 | tf_op jit(solution)/shard_map/ppermute | solution.py:22
  15.8 7.0 %collective-permute-start.1 = (bf16[128,256]{0,1:T(8,128)(2,1)S(1)}, bf16[128,256]{0,1:T(8,128)(2,1)S(1)}, u32[]{:S(2)}, u32[]{:S(2)}) collective-permute-start(bf16[128,256]{0,1:T(8,128)(2,1)S(1)} %collective-permute-done), channel_id=1, source_target_pairs={{0,4},{4,8},{8,12},{12,16},{16,20},{20,24},{24,28},{28,0},{1,5},{5... | collective-permute-start | bytes 196616 | tf_op jit(solution)/shard_map/ppermute | solution.py:22
  22.8 7.0 %collective-permute-start.2 = (bf16[128,256]{0,1:T(8,128)(2,1)S(1)}, bf16[128,256]{0,1:T(8,128)(2,1)S(1)}, u32[]{:S(2)}, u32[]{:S(2)}) collective-permute-start(bf16[128,256]{0,1:T(8,128)(2,1)S(1)} %collective-permute-done.1), channel_id=1, source_target_pairs={{0,4},{4,8},{8,12},{12,16},{16,20},{20,24},{24,28},{28,0},{1,5},{5... | collective-permute-start | bytes 196616 | tf_op jit(solution)/shard_map/ppermute | solution.py:22
  29.8 7.0 %collective-permute-start.3 = (bf16[128,256]{0,1:T(8,128)(2,1)S(1)}, bf16[128,256]{0,1:T(8,128)(2,1)S(1)}, u32[]{:S(2)}, u32[]{:S(2)}) collective-permute-start(bf16[128,256]{0,1:T(8,128)(2,1)S(1)} %collective-permute-done.2), channel_id=1, source_target_pairs={{0,4},{4,8},{8,12},{12,16},{16,20},{20,24},{24,28},{28,0},{1,5},{5... | collective-permute-start | bytes 196616 | tf_op jit(solution)/shard_map/ppermute | solution.py:22
  36.7 7.3 %collective-permute-start.4 = (bf16[128,256]{0,1:T(8,128)(2,1)S(1)}, bf16[128,256]{0,1:T(8,128)(2,1)S(1)}, u32[]{:S(2)}, u32[]{:S(2)}) collective-permute-start(bf16[128,256]{0,1:T(8,128)(2,1)S(1)} %collective-permute-done.3), channel_id=1, source_target_pairs={{0,4},{4,8},{8,12},{12,16},{16,20},{20,24},{24,28},{28,0},{1,5},{5... | collective-permute-start | bytes 196616 | tf_op jit(solution)/shard_map/ppermute | solution.py:22
  44.0 7.0 %collective-permute-start.5 = (bf16[128,256]{0,1:T(8,128)(2,1)S(1)}, bf16[128,256]{0,1:T(8,128)(2,1)S(1)}, u32[]{:S(2)}, u32[]{:S(2)}) collective-permute-start(bf16[128,256]{0,1:T(8,128)(2,1)S(1)} %collective-permute-done.4), channel_id=1, source_target_pairs={{0,4},{4,8},{8,12},{12,16},{16,20},{20,24},{24,28},{28,0},{1,5},{5... | collective-permute-start | bytes 196616 | tf_op jit(solution)/shard_map/ppermute | solution.py:22
  51.0 7.0 %collective-permute-start.6 = (bf16[128,256]{0,1:T(8,128)(2,1)S(1)}, bf16[128,256]{0,1:T(8,128)(2,1)S(1)}, u32[]{:S(2)}, u32[]{:S(2)}) collective-permute-start(bf16[128,256]{0,1:T(8,128)(2,1)S(1)} %collective-permute-done.5), channel_id=1, source_target_pairs={{0,4},{4,8},{8,12},{12,16},{16,20},{20,24},{24,28},{28,0},{1,5},{5... | collective-permute-start | bytes 196616 | tf_op jit(solution)/shard_map/ppermute | solution.py:22
  58.5 0.7 copy-start
Sparse Core Ops, SparseCore 0:
  126.2 75.4 all-reduce.3

commit v2 on v0

--- a/solution.py
+++ b/solution.py
@@ -2,13 +2,14 @@
 import jax.numpy as jnp
 from jax import lax
 from jax.sharding import PartitionSpec as P
+from jax.lax import all_gather
 
 MB_DEV = 4
 
 
 def spread(value, axis, root):
     mine = lax.axis_index(axis) == root
-    return lax.psum(jnp.where(mine, value, jnp.zeros_like(value)), axis)
+    return jnp.sum(all_gather(jnp.where(mine, value, jnp.zeros_like(value)), axis), axis=0)
 
 
 def body(three_index, slot_pair, coeff, occ_mask):

time: 193 us -> 262 us (1.36)
  waiting for transfers between devices: 75.8 us -> 141 us
  other arithmetic: 3.19 us -> 9.17 us
    all_gather x0 -> x2, waiting for transfers between devices: none -> 140 us  [spread(): all_gather(jnp.where(mine, value, jnp.zeros_like(value)), axis)]
    psum x1 -> x0, waiting for transfers between devices: 75.7 us -> none  [spread(): return lax.psum(jnp.where(mine, value, jnp.zeros_like(value)), axis)]
    reduce_sum x0 -> x2, other arithmetic: none -> 5.88 us  [spread(): jnp.sum(all_gather(jnp.where(mine, value, jnp.zeros_like(value)), axis),...]
  transfers between devices with their start and end apart: 1 -> 2, of which waited for: 1 -> 2; matrix products, arithmetic and copies ran while one was open for 0% -> 1% of each run, Pallas kernels for 0% -> 0%
where the time goes in v2:
time: 262 us; the launch traced here: 261 us
  waiting for transfers between devices  141 us (54%)
  blocking collectives  79.6 us (30%)
  between operations  13.5 us (5%)
  loops' own time  9.75 us (4%)
  other arithmetic  9.17 us (4%)
  matrix products  4.81 us (2%)
  local copies, waits for them, and re-layouts  3.76 us (1%)
    all_gather x2, waiting for transfers between devices, spread(): all_gather(jnp.where(mine, value, jnp.zeros_like(value)), axis)  140 us
    psum x1, blocking collectives, body(): mu_half = lax.psum(partial_value, 'col').astype(jnp.bfloat16)  50.1 us
    all_gather x1, blocking collectives, body(): gathered = lax.all_gather(coeff, 'row', axis=0, tiled=True)  29.6 us
    another operation x1, loops' own time, body(): partial_value = lax.fori_loop(0, live_count, add_slot, partial_value)  9.75 us
    reduce_sum x2, other arithmetic, spread(): jnp.sum(all_gather(jnp.where(mine, value, jnp.zeros_like(value)), axis),...  5.88 us
  transfers between devices with their start and end apart: 2, of which 2 were waited for; matrix products, arithmetic and copies ran while one was open for 1% of the time, Pallas kernels for 0%

profile of v2, /device:TPU:0, one launch (start us, length us, event | category | flops | bytes accessed | tf_op | source)
XLA Modules:
  0.0 261.3 jit_solution(12359686313882612836)
XLA Ops:
  6.5 1.4 fusion.10
  8.0 0.7 convert_element_type.17
  8.7 0.9 copy.5
  9.6 29.6 %all_gather.15 = bf16[1024,256]{0,1:T(8,128)(2,1)S(1)} all-gather(bf16[128,256]{0,1:T(8,128)(2,1)S(1)} %copy.5), channel_id=1, replica_groups=mesh['row'=8,'col'=4] {'row'}, dimensions={0}, use_global_device_ids=true | all-gather | bytes 589824 | tf_op jit(solution)/shard_map/all_gather | solution.py:19
  39.5 15.5 %while.12 = (s32[]{:T(128)}, f32[512,2,256]{2,0,1:T(8,128)S(1)}, s32[]{:T(128)}, s32[8]{0:T(128)S(1)}, bf16[1024,256]{0,1:T(8,128)(2,1)S(1)}, /*index=5*/bf16[8,...) while((s32[]{:T(128)}, f32[512,2,256]{2,0,1:T(8,128)S(1)}, ...), condition=%wide.region_2.3_spmd, body=%wide.region_1.2_spmd.sunk | while | flops 16842784 | bytes 2753002 | solution.py:43
  40.2 0.6 dynamic_slice.40
  43.1 0.1 copy.14
  43.2 1.0 fusion.19
  44.2 0.1 copy.15
  45.1 0.6 dynamic_slice.40
  48.0 0.1 copy.14
  48.1 1.0 fusion.19
  49.2 0.1 copy.15
  50.0 0.6 dynamic_slice.40
  53.0 1.0 fusion.19
  54.1 0.1 copy.15
  55.0 50.1 %all-reduce.1 = bf16[512,2,256]{2,0,1:T(8,128)(2,1)S(1)} all-reduce(f32[512,2,256]{2,0,1:T(8,128)S(1)} %get-tuple-element.88), channel_id=1, replica_groups=mesh['row'=8,'col'=4] {'col'}, use_global_device_ids=true, to_apply=%region_3.4 | all-reduce | flops 262144 | bytes 1572864 | tf_op jit(solution)/shard_map/psum | solution.py:46
  105.0 1.1 broadcast_select_fusion.1
  106.2 0.7 all-gather.7.cloned.1.call-update
  106.9 69.4 %all-gather.5.cloned.1.call-done = bf16[4096,2,256]{2,0,1:T(8,128)(2,1)} async-done(((bf16[512,2,256]{2,0,1:T(8,128)(2,1)}), bf16[4096,2,256]{2,0,1:T(8,128)(2,1)}) %all-gather.5.cloned.1.call-update) | async-done | bytes 4194320 | tf_op jit(solution)/shard_map/all_gather | solution.py:12
  176.3 2.9 %reduce_sum.34 = bf16[512,2,256]{2,0,1:T(8,128)(2,1)S(1)} reduce(bf16[8,512,2,256]{3,1,0,2:T(8,128)(2,1)} %bitcast.35, bf16[]{:T(256)} %constant.87.clone.1), dimensions={0}, to_apply=%region_4.5 | reduce | flops 1835008 | bytes 4718594 | tf_op jit(solution)/shard_map/reduce_sum | solution.py:12
  179.3 70.6 %all-gather.7.cloned.1.call-done = bf16[4096,2,256]{2,0,1:T(8,128)(2,1)} async-done(((bf16[512,2,256]{2,0,1:T(8,128)(2,1)}), bf16[4096,2,256]{2,0,1:T(8,128)(2,1)}) %all-gather.7.cloned.1.call-update) | async-done | bytes 4194320 | tf_op jit(solution)/shard_map/all_gather | solution.py:12
  249.8 2.9 %reduce_sum.35 = bf16[512,2,256]{2,0,1:T(8,128)(2,1)S(1)} reduce(bf16[8,512,2,256]{3,1,0,2:T(8,128)(2,1)} %bitcast.36, bf16[]{:T(256)} %constant.87.clone.1), dimensions={0}, to_apply=%region_5.6 | reduce | flops 1835008 | bytes 4718594 | tf_op jit(solution)/shard_map/reduce_sum | solution.py:12
  252.8 1.7 fusion.6
  (15 shorter events, 0.6 us)
Async XLA Ops:
  6.5 32.9 %copy-start = (s32[1,1,8]{2,1,0:T(1,128)S(1)}, s32[1,1,8]{2,1,0:T(1,128)}, u32[]{:S(2)}) copy-start(s32[1,1,8]{2,1,0:T(1,128)} %param.7) | copy-start | bytes 100
  6.5 169.8 %all-gather.5.cloned.1.call-start = ((), (), s32[]{:S(2)}) async-start(), calls=%async_computation | async-start | bytes 4718592 | tf_op jit(solution)/shard_map/all_gather | solution.py:12
  106.1 143.7 %all-gather.7.cloned.1.call-start = ((), (), s32[]{:S(2)}) async-start(), calls=%async_computation.1 | async-start | bytes 4718592 | tf_op jit(solution)/shard_map/all_gather | solution.py:12
Sparse Core Ops, SparseCore 0:
  106.3 70.0 all-gather.4
  178.5 71.2 all-gather.6
